TPU v7x, 32 devices: a whole 2x2x4 slice. The times are simulated.
32 devices in a mesh: dp: 8 (over y, x, core), tensor: 4 (over z).
Axes of the slice: x: 2, y: 2, z: 4, core: 2. Of those that a mesh axis runs over, the one named last changes fastest.
Arguments:
- tokens: bfloat16 [8192, 2048], P(('dp', 'tensor')), may hold values from -6 to 6
- positions: int32 [8192], P('dp'), may hold values from 0 to 1023, as said below
- norm_gain: float32 [2, 2, 2048], replicated, may hold values from 0.25 to 1.75
- norm_bias: float32 [2, 2, 2048], replicated, may hold values from -3 to 3
- w_qkv: bfloat16 [2, 2048, 3, 2048], P(None, 'dp', None, 'tensor'), may hold values from -0.125 to 0.125
- b_qkv: float32 [2, 3, 2048], replicated, may hold values from -3 to 3
- w_out: bfloat16 [2, 2048, 2048], P(None, 'tensor', 'dp'), may hold values from -0.5 to 0.5
- w_gate_up: bfloat16 [2, 2048, 2, 5632], P(None, 'dp', None, 'tensor'), may hold values from -0.125 to 0.125
- w_down: bfloat16 [2, 5632, 2048], P(None, 'tensor', 'dp'), may hold values from -0.078125 to 0.078125
- cotangent: bfloat16 [8192, 2048], P(('dp', 'tensor')), may hold values from -6 to 6
Outputs:
- activations: bfloat16 [8192, 2048], P(('dp', 'tensor'))
- input_grad: float32 [8192, 2048], P(('dp', 'tensor'))
- gain_grad: float32 [2, 2, 2048], replicated
- norm_bias_grad: float32 [2, 2, 2048], replicated
- qkv_grad: float32 [2, 2048, 3, 2048], P(None, 'dp', None, 'tensor')
- qkv_bias_grad: float32 [2, 3, 2048], replicated
- out_grad: float32 [2, 2048, 2048], P(None, 'tensor', 'dp')
- gate_up_grad: float32 [2, 2048, 2, 5632], P(None, 'dp', None, 'tensor')
- down_grad: float32 [2, 5632, 2048], P(None, 'tensor', 'dp')
Inputs may be any that keep to these rules, and one draw needn't show every extreme that they name: positions[i] counts the tokens before i in its document; documents lie end to end in the sequences of 1024 tokens, so the first token of a sequence has 0 and every other token has 0 or one more than the token before it.
All inputs are finite; a program needn't handle non-finite values.
Results may differ from a plain program's by a relative error of at most 0.023.
Values may be sent and summed in bfloat16 or wider, within the bound.
A program may use at most 320 MiB of HBM per device.

v0:
```python
import math
import jax
import jax.numpy as jnp
from jax import lax
from jax.sharding import PartitionSpec as P

HD = 64
ROT = 16
LAYERS = 2
norm_eps = 1e-05
theta_log = math.log(10000.0)
masked_score = -1e30
contract_rows = (((0,), (0,)), ((), ()))
contract_cols = (((1,), (1,)), ((), ()))


def norm_parts(hidden):
    average = jnp.mean(hidden, axis=-1, keepdims=True)
    centred = hidden - average
    variance = jnp.mean(centred * centred, axis=-1, keepdims=True)
    inverse = lax.rsqrt(variance + norm_eps)
    return (centred * inverse, inverse)


def norm_back(grad_normed, scaled, inverse, norm_weight):
    weighted = grad_normed * norm_weight
    first_mean = jnp.mean(weighted, axis=-1, keepdims=True)
    second_mean = jnp.mean(weighted * scaled, axis=-1, keepdims=True)
    grad_input = inverse * (weighted - first_mean - scaled * second_mean)
    return (grad_input, jnp.sum(grad_normed * scaled, axis=0), jnp.sum(grad_normed, axis=0))


def rotary_tables(positions):
    half_rot = ROT // 2
    frequency = jnp.exp(-(jnp.arange(half_rot, dtype=jnp.float32) * 2.0 / ROT) * theta_log)
    angles = positions.astype(jnp.float32)[:, None] * frequency[None, :]
    return (jnp.cos(angles)[:, None, :], jnp.sin(angles)[:, None, :])


def rotate(values, cos_table, sin_table):
    half_rot = ROT // 2
    first_half = values[..., :half_rot]
    second_half = values[..., half_rot:ROT]
    return jnp.concatenate(
        [
            first_half * cos_table - second_half * sin_table,
            second_half * cos_table + first_half * sin_table,
            values[..., ROT:],
        ],
        axis=-1,
    )


def inner_rows(left, right):
    return lax.dot_general(left, right, contract_rows, preferred_element_type=jnp.float32)


def inner_cols(left, right):
    return lax.dot_general(left, right, contract_cols, preferred_element_type=jnp.float32)


def block_scores(queries, key_rows, positions, number, block_rows, score_scale):
    seq_len = key_rows.shape[0]
    row_start = number * block_rows
    query_block = lax.dynamic_slice_in_dim(queries, row_start, block_rows, 0)
    scores = (
        jnp.einsum("qhd,khd->hqk", query_block, key_rows, preferred_element_type=jnp.float32)
        * score_scale
    )
    row_index = row_start + jnp.arange(block_rows, dtype=jnp.int32)
    first_key = row_index - lax.dynamic_slice_in_dim(positions, row_start, block_rows, 0)
    columns = jnp.arange(seq_len, dtype=jnp.int32)
    allowed = (columns[None, :] <= row_index[:, None]) & (columns[None, :] >= first_key[:, None])
    return (query_block, allowed, jnp.where(allowed[None], scores, masked_score))


def attend_forward(queries, key_rows, values, positions, score_scale):
    seq_len = queries.shape[0]
    block_rows = min(512, seq_len)

    def one_block(number):
        query_block, allowed, scores = block_scores(
            queries, key_rows, positions, number, block_rows, score_scale
        )
        row_max = jnp.max(scores, axis=-1, keepdims=True)
        shifted = jnp.exp(scores - row_max)
        row_sum = jnp.sum(shifted, axis=-1, keepdims=True)
        weights_low = (shifted / row_sum).astype(jnp.bfloat16)
        block_out = jnp.einsum(
            "hqk,khd->qhd", weights_low, values, preferred_element_type=jnp.float32
        )
        return (block_out, row_max + jnp.log(row_sum))

    block_outs, logsums = lax.map(one_block, jnp.arange(seq_len // block_rows, dtype=jnp.int32))
    return (block_outs.reshape(seq_len, -1), logsums)


def attend_back(queries, key_rows, values, positions, logsums, grad_attended, score_scale):
    seq_len = queries.shape[0]
    block_rows = min(512, seq_len)

    def one_block(totals, inputs):
        grad_keys, grad_values = totals
        number, logsum = inputs
        query_block, allowed, scores = block_scores(
            queries, key_rows, positions, number, block_rows, score_scale
        )
        softmax_rows = jnp.exp(scores - logsum)
        grad_block = lax.dynamic_slice_in_dim(grad_attended, number * block_rows, block_rows, 0)
        grad_probs = jnp.einsum(
            "qhd,khd->hqk", grad_block, values, preferred_element_type=jnp.float32
        )
        grad_values = grad_values + jnp.einsum(
            "hqk,qhd->khd",
            softmax_rows.astype(jnp.bfloat16),
            grad_block,
            preferred_element_type=jnp.float32,
        )
        row_inner = jnp.sum(softmax_rows * grad_probs, axis=-1, keepdims=True)
        grad_scores = jnp.where(allowed[None], softmax_rows * (grad_probs - row_inner), 0.0).astype(
            jnp.bfloat16
        )
        grad_query = (
            jnp.einsum("hqk,khd->qhd", grad_scores, key_rows, preferred_element_type=jnp.float32)
            * score_scale
        )
        grad_keys = (
            grad_keys
            + jnp.einsum(
                "hqk,qhd->khd", grad_scores, query_block, preferred_element_type=jnp.float32
            )
            * score_scale
        )
        return ((grad_keys, grad_values), grad_query)

    empty_grad = jnp.zeros(key_rows.shape, jnp.float32)
    numbers = jnp.arange(seq_len // block_rows, dtype=jnp.int32)
    (grad_keys, grad_values), grad_queries = lax.scan(
        one_block, (empty_grad, empty_grad), (numbers, logsums)
    )
    return (grad_queries.reshape(queries.shape), grad_keys, grad_values)


def per_device(
    tokens, positions, norm_gain, norm_bias, w_qkv, b_qkv, w_out, w_gate_up, w_down, cotangent
):
    tensor_rank = lax.axis_index("tensor")
    width_local = w_qkv.shape[3]
    heads_local = width_local // HD
    ff_local = w_gate_up.shape[3]
    local_rows = tokens.shape[0]
    seq_len = positions.shape[0]
    score_scale = 1.0 / math.sqrt(HD)
    cos_table, sin_table = rotary_tables(positions)
    hidden = tokens.astype(jnp.float32)
    kept_state = []
    for layer_index in range(LAYERS):
        gathered = (
            lax.all_gather(w_qkv[layer_index], "dp", axis=0, tiled=True),
            lax.all_gather(w_out[layer_index], "dp", axis=1, tiled=True),
            lax.all_gather(w_gate_up[layer_index], "dp", axis=0, tiled=True),
            lax.all_gather(w_down[layer_index], "dp", axis=1, tiled=True),
        )
        full_qkv, full_out, full_gu, full_down = gathered
        scaled_a, inverse_a = norm_parts(hidden)
        normed_a = (scaled_a * norm_gain[layer_index, 0] + norm_bias[layer_index, 0]).astype(
            jnp.bfloat16
        )
        rows_a = lax.all_gather(normed_a, "tensor", axis=0, tiled=True)
        bias_local = lax.dynamic_slice_in_dim(
            b_qkv[layer_index], tensor_rank * width_local, width_local, 1
        )
        mixed = jnp.dot(
            rows_a,
            full_qkv.reshape(full_qkv.shape[0], 3 * width_local),
            preferred_element_type=jnp.float32,
        ) + bias_local.reshape(3 * width_local)
        mixed = mixed.reshape(seq_len, 3, heads_local, HD)
        queries = rotate(mixed[:, 0], cos_table, sin_table).astype(jnp.bfloat16)
        key_rows = rotate(mixed[:, 1], cos_table, sin_table).astype(jnp.bfloat16)
        values = mixed[:, 2].astype(jnp.bfloat16)
        attended, logsums = attend_forward(queries, key_rows, values, positions, score_scale)
        attended = attended.astype(jnp.bfloat16)

        def project_attn(row_start, row_count, source=attended, weight=full_out):
            return jnp.dot(source, weight, preferred_element_type=jnp.float32)

        branch_a = lax.psum_scatter(
            project_attn(jnp.int32(0), local_rows * lax.axis_size("tensor")).astype(jnp.bfloat16),
            "tensor",
            scatter_dimension=0,
            tiled=True,
        ).astype(jnp.float32)
        hidden_mid = hidden + branch_a
        scaled_b, inverse_b = norm_parts(hidden_mid)
        normed_b = (scaled_b * norm_gain[layer_index, 1] + norm_bias[layer_index, 1]).astype(
            jnp.bfloat16
        )
        rows_b = lax.all_gather(normed_b, "tensor", axis=0, tiled=True)
        gate_up = jnp.dot(
            rows_b,
            full_gu.reshape(full_gu.shape[0], 2 * ff_local),
            preferred_element_type=jnp.float32,
        ).reshape(seq_len, 2, ff_local)
        activated = (jax.nn.silu(gate_up[:, 0]) * gate_up[:, 1]).astype(jnp.bfloat16)

        def project_mlp(row_start, row_count, source=activated, weight=full_down):
            return jnp.dot(source, weight, preferred_element_type=jnp.float32)

        hidden = hidden_mid + lax.psum_scatter(
            project_mlp(jnp.int32(0), local_rows * lax.axis_size("tensor")).astype(jnp.bfloat16),
            "tensor",
            scatter_dimension=0,
            tiled=True,
        ).astype(jnp.float32)
        kept_state.append(
            (
                gathered,
                scaled_a,
                inverse_a,
                rows_a,
                queries,
                key_rows,
                values,
                logsums,
                attended,
                scaled_b,
                inverse_b,
                rows_b,
                gate_up,
                activated,
            )
        )
    activations = hidden.astype(jnp.bfloat16)
    grad = cotangent.astype(jnp.float32)
    weight_parts = [None] * LAYERS
    gain_rows = [None] * LAYERS
    shift_rows = [None] * LAYERS
    qkv_shift_rows = [None] * LAYERS
    for layer_index in reversed(range(LAYERS)):
        (
            gathered,
            scaled_a,
            inverse_a,
            rows_a,
            queries,
            key_rows,
            values,
            logsums,
            attended,
            scaled_b,
            inverse_b,
            rows_b,
            gate_up,
            activated,
        ) = kept_state[layer_index]
        full_qkv, full_out, full_gu, full_down = (
            lax.all_gather(w_qkv[layer_index], "dp", axis=0, tiled=True),
            lax.all_gather(w_out[layer_index], "dp", axis=1, tiled=True),
            lax.all_gather(w_gate_up[layer_index], "dp", axis=0, tiled=True),
            lax.all_gather(w_down[layer_index], "dp", axis=1, tiled=True),
        )
        grad_rows_b = lax.all_gather(grad.astype(jnp.bfloat16), "tensor", axis=0, tiled=True)
        grad_down_weight = inner_rows(activated, grad_rows_b)
        grad_act = inner_cols(grad_rows_b, full_down)
        gate_part = gate_up[:, 0]
        up_part = gate_up[:, 1]
        sigmoid_gate = jax.nn.sigmoid(gate_part)
        grad_gate = grad_act * up_part * sigmoid_gate * (1.0 + gate_part * (1.0 - sigmoid_gate))
        grad_up = grad_act * jax.nn.silu(gate_part)
        grad_gate_up = (
            jnp.stack([grad_gate, grad_up], axis=1)
            .astype(jnp.bfloat16)
            .reshape(seq_len, 2 * ff_local)
        )
        grad_gu_weight = inner_rows(rows_b, grad_gate_up).reshape(full_gu.shape)
        flat_gu = full_gu.reshape(full_gu.shape[0], 2 * ff_local)

        def back_mlp(row_start, row_count, source=grad_gate_up, weight=flat_gu):
            return inner_cols(source, weight)

        grad_normed_b = lax.psum_scatter(
            back_mlp(jnp.int32(0), local_rows * lax.axis_size("tensor")).astype(jnp.bfloat16),
            "tensor",
            scatter_dimension=0,
            tiled=True,
        ).astype(jnp.float32)
        grad_in_b, gain_b, shift_b = norm_back(
            grad_normed_b, scaled_b, inverse_b, norm_gain[layer_index, 1]
        )
        grad = grad + grad_in_b
        grad_rows_a = lax.all_gather(grad.astype(jnp.bfloat16), "tensor", axis=0, tiled=True)
        grad_out_weight = inner_rows(attended, grad_rows_a)
        grad_attended = inner_cols(grad_rows_a, full_out).astype(jnp.bfloat16)
        grad_attended = grad_attended.reshape(seq_len, heads_local, HD)
        grad_queries, grad_keys, grad_values = attend_back(
            queries, key_rows, values, positions, logsums, grad_attended, score_scale
        )
        grad_queries = rotate(grad_queries, cos_table, -sin_table)
        grad_keys = rotate(grad_keys, cos_table, -sin_table)
        grad_mixed = jnp.stack([grad_queries, grad_keys, grad_values], axis=1)
        grad_mixed = grad_mixed.reshape(seq_len, 3 * width_local).astype(jnp.bfloat16)
        qkv_shift_local = jnp.sum(grad_mixed, axis=0, dtype=jnp.float32).reshape(3, width_local)
        qkv_shift_rows[layer_index] = lax.dynamic_update_slice(
            jnp.zeros((3, b_qkv.shape[2]), jnp.float32),
            qkv_shift_local,
            (jnp.int32(0), tensor_rank * width_local),
        )
        grad_qkv_weight = inner_rows(rows_a, grad_mixed).reshape(full_qkv.shape)
        flat_qkv = full_qkv.reshape(full_qkv.shape[0], 3 * width_local)

        def back_attn(row_start, row_count, source=grad_mixed, weight=flat_qkv):
            return inner_cols(source, weight)

        grad_normed_a = lax.psum_scatter(
            back_attn(jnp.int32(0), local_rows * lax.axis_size("tensor")).astype(jnp.bfloat16),
            "tensor",
            scatter_dimension=0,
            tiled=True,
        ).astype(jnp.float32)
        grad_in_a, gain_a, shift_a = norm_back(
            grad_normed_a, scaled_a, inverse_a, norm_gain[layer_index, 0]
        )
        grad = grad + grad_in_a
        gain_rows[layer_index] = jnp.stack([gain_a, gain_b])
        shift_rows[layer_index] = jnp.stack([shift_a, shift_b])
        weight_parts[layer_index] = (
            lax.psum_scatter(
                grad_qkv_weight.astype(jnp.bfloat16), "dp", scatter_dimension=0, tiled=True
            ).astype(jnp.float32),
            lax.psum_scatter(
                grad_out_weight.astype(jnp.bfloat16), "dp", scatter_dimension=1, tiled=True
            ).astype(jnp.float32),
            lax.psum_scatter(
                grad_gu_weight.astype(jnp.bfloat16), "dp", scatter_dimension=0, tiled=True
            ).astype(jnp.float32),
            lax.psum_scatter(
                grad_down_weight.astype(jnp.bfloat16), "dp", scatter_dimension=1, tiled=True
            ).astype(jnp.float32),
        )
    stack_qkv = jnp.stack([weight_parts[number][0] for number in range(LAYERS)])
    stack_out = jnp.stack([weight_parts[number][1] for number in range(LAYERS)])
    stack_gu = jnp.stack([weight_parts[number][2] for number in range(LAYERS)])
    stack_down = jnp.stack([weight_parts[number][3] for number in range(LAYERS)])
    gain_grad, norm_bias_grad, qkv_bias_grad = lax.psum(
        (jnp.stack(gain_rows), jnp.stack(shift_rows), jnp.stack(qkv_shift_rows)), ("dp", "tensor")
    )
    return (
        activations,
        grad,
        gain_grad,
        norm_bias_grad,
        stack_qkv,
        qkv_bias_grad,
        stack_out,
        stack_gu,
        stack_down,
    )


def solution(mesh):
    in_specs = (
        P(("dp", "tensor"), None),
        P("dp"),
        P(),
        P(),
        P(None, "dp", None, "tensor"),
        P(),
        P(None, "tensor", "dp"),
        P(None, "dp", None, "tensor"),
        P(None, "tensor", "dp"),
        P(("dp", "tensor"), None),
    )
    out_specs = (
        P(("dp", "tensor"), None),
        P(("dp", "tensor"), None),
        P(),
        P(),
        P(None, "dp", None, "tensor"),
        P(),
        P(None, "tensor", "dp"),
        P(None, "dp", None, "tensor"),
        P(None, "tensor", "dp"),
    )
    return jax.shard_map(
        per_device, mesh=mesh, in_specs=in_specs, out_specs=out_specs, check_vma=False
    )
```

profile of v0, /device:TPU:1, one launch (start us, length us, event | category | flops | bytes accessed | tf_op | source)
XLA Modules:
  0.0 2722.3 jit_solution(6625782385930977792)
XLA Ops:
  20.9 78.1 %all-gather.25.cloned.1.call-done = bf16[1024,2048]{1,0:T(8,128)(2,1)} async-done(((bf16[256,2048]{1,0:T(8,128)(2,1)}), bf16[1024,2048]{1,0:T(8,128)(2,1)}) %all-gather.25.cloned.1.call-update) | async-done | bytes 4194320 | tf_op jit(solution)/shard_map/all_gather | solution.py:169
  99.0 48.1 %all-gather.41.cloned.1.call-done = bf16[1,2048,3,512]{1,3,2,0:T(8,128)(2,1)} async-done(((bf16[1,256,3,512]{1,3,2,0:T(8,128)(2,1)}), bf16[1,2048,3,512]{1,3,2,0:T(8,128)(2,1)}) %all-gather.41.cloned.1.call-update) | async-done | bytes 6291472 | tf_op jit(solution)/shard_map/all_gather | solution.py:159
  171.9 31.3 %while.54 = (s32[]{:T(128)}, bf16[2,512,8,64]{1,3,2,0:T(8,128)(2,1)}, f32[2,8,512,1]{2,1,3,0:T(8,128)S(1)}, s32[2]{0:T(128)S(1)}, s32[1024]{0:T(1024)S(1)}, /*in...) while((s32[]{:T(128)}, ...), condition=%wide.region_5.6_spmd, body=%wide.region_2.5_spmd.sunk | while | flops 1125643264 | bytes 64628996 | solution.py:94
  219.9 70.5 %reduce-scatter.17.cloned.1.call-done = bf16[256,2048]{1,0:T(8,128)(2,1)} async-done(((bf16[1024,2048]{1,0:T(8,128)(2,1)}), bf16[256,2048]{1,0:T(8,128)(2,1)}) %reduce-scatter.17.cloned.1.call-update) | async-done | bytes 1048592 | tf_op jit(solution)/shard_map/reduce_scatter | solution.py:188
  298.2 63.4 %all-gather.45.cloned.1.call-done = bf16[1,2048,2,1408]{3,1,2,0:T(8,128)(2,1)} async-done(((bf16[1,256,2,1408]{3,1,2,0:T(8,128)(2,1)}), bf16[1,2048,2,1408]{3,1,2,0:T(8,128)(2,1)}) %all-gather.45.cloned.1.call-update) | async-done | bytes 11534352 | tf_op jit(solution)/shard_map/all_gather | solution.py:161
  377.3 66.7 %all-gather.27.cloned.1.call-done = bf16[1024,2048]{1,0:T(8,128)(2,1)} async-done(((bf16[256,2048]{1,0:T(8,128)(2,1)}), bf16[1024,2048]{1,0:T(8,128)(2,1)}) %all-gather.27.cloned.1.call-update) | async-done | bytes 4194320 | tf_op jit(solution)/shard_map/all_gather | solution.py:199
  444.0 17.3 fusion.96
  468.2 21.7 all-gather.47.cloned.1.call-done
  503.3 74.1 %reduce-scatter.19.cloned.1.call-done = bf16[256,2048]{1,0:T(8,128)(2,1)} async-done(((bf16[1024,2048]{1,0:T(8,128)(2,1)}), bf16[256,2048]{1,0:T(8,128)(2,1)}) %reduce-scatter.19.cloned.1.call-update) | async-done | bytes 1048592 | tf_op jit(solution)/shard_map/reduce_scatter | solution.py:210
  583.4 43.5 %all-gather.49.cloned.1.call-done = bf16[1,2048,3,512]{1,3,2,0:T(8,128)(2,1)} async-done(((bf16[1,256,3,512]{1,3,2,0:T(8,128)(2,1)}), bf16[1,2048,3,512]{1,3,2,0:T(8,128)(2,1)}) %all-gather.49.cloned.1.call-update) | async-done | bytes 6291472 | tf_op jit(solution)/shard_map/all_gather | solution.py:159
  626.9 82.4 %all-gather.29.cloned.1.call-done = bf16[1024,2048]{1,0:T(8,128)(2,1)} async-done(((bf16[256,2048]{1,0:T(8,128)(2,1)}), bf16[1024,2048]{1,0:T(8,128)(2,1)}) %all-gather.29.cloned.1.call-update) | async-done | bytes 4194320 | tf_op jit(solution)/shard_map/all_gather | solution.py:169
  735.0 33.6 %while.55 = (s32[]{:T(128)}, bf16[2,512,8,64]{1,3,2,0:T(8,128)(2,1)S(1)}, f32[2,8,512,1]{2,1,3,0:T(8,128)S(1)}, s32[2]{0:T(128)S(1)}, s32[1024]{0:T(1024)S(1)}, ...) while((s32[]{:T(128)}, ...), condition=%wide.region_15.16_spmd, body=%wide.region_12.15_spmd.sunk | while | flops 1125643264 | bytes 56240328 | solution.py:94
  779.1 72.6 %reduce-scatter.21.cloned.1.call-done = bf16[256,2048]{1,0:T(8,128)(2,1)} async-done(((bf16[1024,2048]{1,0:T(8,128)(2,1)}), bf16[256,2048]{1,0:T(8,128)(2,1)}) %reduce-scatter.21.cloned.1.call-update) | async-done | bytes 1048592 | tf_op jit(solution)/shard_map/reduce_scatter | solution.py:188
  857.2 65.2 %all-gather.53.cloned.1.call-done = bf16[1,2048,2,1408]{3,1,2,0:T(8,128)(2,1)} async-done(((bf16[1,256,2,1408]{3,1,2,0:T(8,128)(2,1)}), bf16[1,2048,2,1408]{3,1,2,0:T(8,128)(2,1)}) %all-gather.53.cloned.1.call-update) | async-done | bytes 11534352 | tf_op jit(solution)/shard_map/all_gather | solution.py:161
  938.0 66.9 %all-gather.31.cloned.1.call-done = bf16[1024,2048]{1,0:T(8,128)(2,1)} async-done(((bf16[256,2048]{1,0:T(8,128)(2,1)}), bf16[1024,2048]{1,0:T(8,128)(2,1)}) %all-gather.31.cloned.1.call-update) | async-done | bytes 4194320 | tf_op jit(solution)/shard_map/all_gather | solution.py:199
  1004.8 18.8 fusion.94
  1023.7 62.0 %all-gather.33.cloned.1.call-done = bf16[1024,2048]{1,0:T(8,128)(2,1)} async-done(((bf16[256,2048]{1,0:T(8,128)(2,1)}), bf16[1024,2048]{1,0:T(8,128)(2,1)}) %all-gather.33.cloned.1.call-update) | async-done | bytes 4194320 | tf_op jit(solution)/shard_map/all_gather | solution.py:263
  1085.7 45.2 %all-gather.55.cloned.1.call-done = bf16[1,1408,2048]{2,1,0:T(8,128)(2,1)} async-done(((bf16[1,1408,256]{2,1,0:T(8,128)(2,1)}), bf16[1,1408,2048]{2,1,0:T(8,128)(2,1)}) %all-gather.55.cloned.1.call-update) | async-done | bytes 5767184 | tf_op jit(solution)/shard_map/all_gather | solution.py:162
  1147.5 16.3 bitcast_convert_fusion.1
  1182.0 58.3 %reduce-scatter.25.cloned.1.call-done = bf16[256,2048]{1,0:T(8,128)(2,1)} async-done(((bf16[1024,2048]{1,0:T(8,128)(2,1)}), bf16[256,2048]{1,0:T(8,128)(2,1)}) %reduce-scatter.25.cloned.1.call-update) | async-done | bytes 1048592 | tf_op jit(solution)/shard_map/reduce_scatter | solution.py:282
  1243.1 76.6 %reduce-scatter.23.cloned.1.call-done = bf16[256,2048]{1,0:T(8,128)(2,1)} async-done(((bf16[1024,2048]{1,0:T(8,128)(2,1)}), bf16[256,2048]{1,0:T(8,128)(2,1)}) %reduce-scatter.23.cloned.1.call-update) | async-done | bytes 1048592 | tf_op jit(solution)/shard_map/reduce_scatter | solution.py:210
  1324.5 81.3 %all-gather.35.cloned.1.call-done = bf16[1024,2048]{1,0:T(8,128)(2,1)} async-done(((bf16[256,2048]{1,0:T(8,128)(2,1)}), bf16[1024,2048]{1,0:T(8,128)(2,1)}) %all-gather.35.cloned.1.call-update) | async-done | bytes 4194320 | tf_op jit(solution)/shard_map/all_gather | solution.py:292
  1414.1 183.7 %while.56 = (s32[]{:T(128)}, f32[1024,8,64]{0,2,1:T(8,128)}, f32[1024,8,64]{0,2,1:T(8,128)S(1)}, f32[2,512,8,64]{1,0,3,2:T(2,128)}, s32[2]{0:T(128)S(1)}, /*inde...) while((s32[]{:T(128)}, f32[1024,8,64]{0,2,1:T(8,128)}, ...), condition=%wide.region_25.26_spmd.clone, body=%wide.region_23.25_spmd.clone.sunk | while | flops 2747542528 | bytes 239134992 | solution.py:138
  1437.5 22.9 fusion.302
  1460.4 23.3 bitcast_add_fusion.8
  1486.1 19.6 dynamic_update_slice.48
  1528.8 22.9 fusion.302
  1551.8 23.9 bitcast_add_fusion.8
  1578.0 19.6 dynamic_update_slice.48
  1618.3 75.4 %reduce-scatter.27.cloned.1.call-done = bf16[256,2048]{1,0:T(8,128)(2,1)} async-done(((bf16[1024,2048]{1,0:T(8,128)(2,1)}), bf16[256,2048]{1,0:T(8,128)(2,1)}) %reduce-scatter.27.cloned.1.call-update) | async-done | bytes 1048592 | tf_op jit(solution)/shard_map/reduce_scatter | solution.py:315
  1699.3 81.4 %all-gather.37.cloned.1.call-done = bf16[1024,2048]{1,0:T(8,128)(2,1)} async-done(((bf16[256,2048]{1,0:T(8,128)(2,1)}), bf16[1024,2048]{1,0:T(8,128)(2,1)}) %all-gather.37.cloned.1.call-update) | async-done | bytes 4194320 | tf_op jit(solution)/shard_map/all_gather | solution.py:263
  1814.0 75.4 %reduce-scatter.29.cloned.1.call-done = bf16[256,2048]{1,0:T(8,128)(2,1)} async-done(((bf16[1024,2048]{1,0:T(8,128)(2,1)}), bf16[256,2048]{1,0:T(8,128)(2,1)}) %reduce-scatter.29.cloned.1.call-update) | async-done | bytes 1048592 | tf_op jit(solution)/shard_map/reduce_scatter | solution.py:282
  1933.9 19.1 convolution_convert_fusion
  1968.5 19.2 convolution_convert_fusion.1
  2010.9 198.1 %while.57 = (s32[]{:T(128)}, f32[1024,8,64]{0,2,1:T(8,128)}, f32[1024,8,64]{0,2,1:T(8,128)}, f32[2,512,8,64]{1,0,3,2:T(2,128)}, s32[2]{0:T(128)S(1)}, /*index=5*...) while((s32[]{:T(128)}, f32[1024,8,64]{0,2,1:T(8,128)}, ...), condition=%wide.region_34.35_spmd.clone, body=%wide.region_32.34_spmd.clone.sunk | while | flops 2747542528 | bytes 239134992 | solution.py:138
  2034.5 27.4 %fusion.315 = f32[1,512,8,64]{1,3,2,0:T(8,128)} fusion(bf16[1024,8,64]{0,2,1:T(8,128)(2,1)S(1)} %get-tuple-element.900, f32[8,512,1024]{2,1,0:T(8,128)} %copy-done.1, f32[8,512,1024]{2,1,0:T(8,128)} %fusion.314, pred[512,1024]{1,0:T(8,128)(4,1)S(1)} %fusion.313), kind=kOutput, calls=%fused_computation.87.clone.1 | convolution fusion | flops 558109696 | bytes 36175872 | tf_op jit(solution)/shard_map/while/body/eval_jaxpr/hqk,khd->qhd/dot_general | solution.py:124
  2061.9 24.7 bitcast_add_fusion.10
  2088.9 19.5 dynamic_update_slice.49
  2135.0 26.6 fusion.315
  2161.6 25.4 bitcast_add_fusion.10
  2189.3 19.7 dynamic_update_slice.49
  2259.2 22.5 reduce-scatter.41.cloned.1.call-done
  2290.9 35.7 %reduce-scatter.39.cloned.1.call-done = bf16[512,256]{1,0:T(8,128)(2,1)} async-done(((bf16[512,2048]{1,0:T(8,128)(2,1)}), bf16[512,256]{1,0:T(8,128)(2,1)}) %reduce-scatter.39.cloned.1.call-update) | async-done | bytes 262160 | tf_op jit(solution)/shard_map/reduce_scatter | solution.py:331
  2326.6 44.5 %reduce-scatter.37.cloned.1.call-done = bf16[512,256]{1,0:T(8,128)(2,1)} async-done(((bf16[512,2048]{1,0:T(8,128)(2,1)}), bf16[512,256]{1,0:T(8,128)(2,1)}) %reduce-scatter.37.cloned.1.call-update) | async-done | bytes 262160 | tf_op jit(solution)/shard_map/reduce_scatter | solution.py:331
  2373.2 77.0 %reduce-scatter.31.cloned.1.call-done = bf16[256,2048]{1,0:T(8,128)(2,1)} async-done(((bf16[1024,2048]{1,0:T(8,128)(2,1)}), bf16[256,2048]{1,0:T(8,128)(2,1)}) %reduce-scatter.31.cloned.1.call-update) | async-done | bytes 1048592 | tf_op jit(solution)/shard_map/reduce_scatter | solution.py:315
  2457.2 58.6 %reduce-scatter.35.cloned.1.call-done = bf16[256,3,512]{2,0,1:T(8,128)(2,1)} async-done(((bf16[2048,3,512]{2,0,1:T(8,128)(2,1)}), bf16[256,3,512]{2,0,1:T(8,128)(2,1)}) %reduce-scatter.35.cloned.1.call-update) | async-done | bytes 786448 | tf_op jit(solution)/shard_map/reduce_scatter | solution.py:328
  2515.8 65.6 %reduce-scatter.33.cloned.1.call-done = bf16[256,3,512]{2,0,1:T(8,128)(2,1)} async-done(((bf16[2048,3,512]{2,0,1:T(8,128)(2,1)}), bf16[256,3,512]{2,0,1:T(8,128)(2,1)}) %reduce-scatter.33.cloned.1.call-update) | async-done | bytes 786448 | tf_op jit(solution)/shard_map/reduce_scatter | solution.py:328
  2584.6 126.3 %all-reduce.3.cloned.1.call-done = (f32[2,2,2048]{2,1,0:T(2,128)}, f32[2,2,2048]{2,1,0:T(2,128)}, f32[2,3,2048]{2,0,1:T(2,128)}) async-done(((f32[2,2,2048]{2,1,0:T(2,128)}, f32[2,2,2048]{2,1,0:T(2,128)}, f32[2,3,2048]{2,0,1:T(2,128)}), (f32[2,2,2048]{2,1,0:T(2,128)}, f32[2,2,2048]{2,1,0:T(2,128)}, f32[2,3,2048]{2,0,1:T(2,128)})) %all-reduce.3.cloned.1.call-update) | async-done | bytes 114704 | tf_op jit(solution)/shard_map/psum | solution.py:345
  (483 shorter events, 594.5 us)
Async XLA Ops:
  7.2 91.8 %all-gather.25.cloned.1.call-start = ((), (), s32[]{:S(2)}) async-start(), calls=%async_computation.16 | async-start | bytes 5242880 | tf_op jit(solution)/shard_map/all_gather | solution.py:169
  16.0 131.1 %all-gather.41.cloned.1.call-start = ((), (), s32[]{:S(2)}) async-start(), calls=%async_computation.40 | async-start | bytes 7077888 | tf_op jit(solution)/shard_map/all_gather | solution.py:159
  18.4 189.1 %all-gather.43.cloned.1.call-start = ((), (), s32[]{:S(2)}) async-start(), calls=%async_computation.41 | async-start | bytes 2359296 | tf_op jit(solution)/shard_map/all_gather | solution.py:160
  19.3 271.1 %reduce-scatter.17.cloned.1.call-start = ((), (), s32[]{:S(2)}) async-start(), calls=%async_computation.17 | async-start | bytes 5242880 | tf_op jit(solution)/shard_map/reduce_scatter | solution.py:188
  20.9 149.5 %copy-start.47 = (f32[1024,8]{0,1:T(8,128)}, f32[1024,8]{0,1:T(8,128)S(1)}, u32[]{:S(2)}) copy-start(f32[1024,8]{0,1:T(8,128)S(1)} %get-tuple-element.487) | copy-start | bytes 98308
  20.9 149.5 %copy-start.61 = (f32[1024,8]{0,1:T(8,128)}, f32[1024,8]{0,1:T(8,128)S(1)}, u32[]{:S(2)}) copy-start(f32[1024,8]{0,1:T(8,128)S(1)} %get-tuple-element.486) | copy-start | bytes 98308
  213.9 147.6 %all-gather.45.cloned.1.call-start = ((), (), s32[]{:S(2)}) async-start(), calls=%async_computation.42 | async-start | bytes 12976128 | tf_op jit(solution)/shard_map/all_gather | solution.py:161
  219.9 224.1 %all-gather.27.cloned.1.call-start = ((), (), s32[]{:S(2)}) async-start(), calls=%async_computation.18 | async-start | bytes 5242880 | tf_op jit(solution)/shard_map/all_gather | solution.py:199
  296.8 193.1 %all-gather.47.cloned.1.call-start = ((), (), s32[]{:S(2)}) async-start(), calls=%async_computation.43 | async-start | bytes 6488064 | tf_op jit(solution)/shard_map/all_gather | solution.py:162
  298.1 279.3 %reduce-scatter.19.cloned.1.call-start = ((), (), s32[]{:S(2)}) async-start(), calls=%async_computation.19 | async-start | bytes 5242880 | tf_op jit(solution)/shard_map/reduce_scatter | solution.py:210
  500.8 126.0 %all-gather.49.cloned.1.call-start = ((), (), s32[]{:S(2)}) async-start(), calls=%async_computation.44 | async-start | bytes 7077888 | tf_op jit(solution)/shard_map/all_gather | solution.py:159
  503.2 77.2 %copy-start.67 = (f32[1,1,2048]{2,1,0:T(1,128)S(1)}, f32[1,1,2048]{2,1,0:T(1,128)}, u32[]{:S(2)}) copy-start(f32[1,1,2048]{2,1,0:T(1,128)} %get-tuple-element.480) | copy-start | bytes 24580
  503.2 77.2 %copy-start.79 = (f32[1,1,2048]{2,1,0:T(1,128)S(1)}, f32[1,1,2048]{2,1,0:T(1,128)}, u32[]{:S(2)}) copy-start(f32[1,1,2048]{2,1,0:T(1,128)} %get-tuple-element.484) | copy-start | bytes 24580
  503.2 206.0 %all-gather.29.cloned.1.call-start = ((), (), s32[]{:S(2)}) async-start(), calls=%async_computation.20 | async-start | bytes 5242880 | tf_op jit(solution)/shard_map/all_gather | solution.py:169
  579.5 141.8 %copy-start.88 = (f32[256]{0:T(256)}, f32[256]{0:T(256)S(1)}, u32[]{:S(2)}) copy-start(f32[256]{0:T(256)S(1)} %add_rsqrt_fusion.1) | copy-start | bytes 3076
  581.9 188.2 %all-gather.51.cloned.1.call-start = ((), (), s32[]{:S(2)}) async-start(), calls=%async_computation.45 | async-start | bytes 2359296 | tf_op jit(solution)/shard_map/all_gather | solution.py:160
  582.6 269.1 %reduce-scatter.21.cloned.1.call-start = ((), (), s32[]{:S(2)}) async-start(), calls=%async_computation.21 | async-start | bytes 5242880 | tf_op jit(solution)/shard_map/reduce_scatter | solution.py:188
  776.4 145.9 %all-gather.53.cloned.1.call-start = ((), (), s32[]{:S(2)}) async-start(), calls=%async_computation.46 | async-start | bytes 12976128 | tf_op jit(solution)/shard_map/all_gather | solution.py:161
  779.1 225.8 %all-gather.31.cloned.1.call-start = ((), (), s32[]{:S(2)}) async-start(), calls=%async_computation.22 | async-start | bytes 5242880 | tf_op jit(solution)/shard_map/all_gather | solution.py:199
  856.0 229.7 %all-gather.33.cloned.1.call-start = ((), (), s32[]{:S(2)}) async-start(), calls=%async_computation.24 | async-start | bytes 5242880 | tf_op jit(solution)/shard_map/all_gather | solution.py:263
  856.6 274.3 %all-gather.55.cloned.1.call-start = ((), (), s32[]{:S(2)}) async-start(), calls=%async_computation.47 | async-start | bytes 6488064 | tf_op jit(solution)/shard_map/all_gather | solution.py:162
  857.1 383.2 %reduce-scatter.25.cloned.1.call-start = ((), (), s32[]{:S(2)}) async-start(), calls=%async_computation.25 | async-start | bytes 5242880 | tf_op jit(solution)/shard_map/reduce_scatter | solution.py:282
  1163.8 156.0 %reduce-scatter.23.cloned.1.call-start = ((), (), s32[]{:S(2)}) async-start(), calls=%async_computation.23 | async-start | bytes 5242880 | tf_op jit(solution)/shard_map/reduce_scatter | solution.py:210
  1181.9 137.9 %copy-start.23 = (bf16[256,2048]{1,0:T(8,128)(2,1)S(1)}, bf16[256,2048]{1,0:T(8,128)(2,1)}, u32[]{:S(2)}) copy-start(bf16[256,2048]{1,0:T(8,128)(2,1)} %param.27) | copy-start | bytes 3145732
  1181.9 223.9 %all-gather.35.cloned.1.call-start = ((), (), s32[]{:S(2)}) async-start(), calls=%async_computation.26 | async-start | bytes 5242880 | tf_op jit(solution)/shard_map/all_gather | solution.py:292
  1324.5 369.3 %reduce-scatter.27.cloned.1.call-start = ((), (), s32[]{:S(2)}) async-start(), calls=%async_computation.27 | async-start | bytes 5242880 | tf_op jit(solution)/shard_map/reduce_scatter | solution.py:315
  1324.5 89.6 %copy-start.58 = (f32[2,8,512,1]{2,1,3,0:T(8,128)S(1)}, f32[2,8,512,1]{2,1,3,0:T(8,128)}, u32[]{:S(2)}) copy-start(f32[2,8,512,1]{2,1,3,0:T(8,128)} %copy-done.57) | copy-start | bytes 98308
  1618.3 162.4 %all-gather.37.cloned.1.call-start = ((), (), s32[]{:S(2)}) async-start(), calls=%async_computation.28 | async-start | bytes 5242880 | tf_op jit(solution)/shard_map/all_gather | solution.py:263
  1699.3 190.2 %reduce-scatter.29.cloned.1.call-start = ((), (), s32[]{:S(2)}) async-start(), calls=%async_computation.29 | async-start | bytes 5242880 | tf_op jit(solution)/shard_map/reduce_scatter | solution.py:282
  1813.9 75.5 %copy-start.87 = (f32[256]{0:T(256)S(1)}, f32[256]{0:T(256)}, u32[]{:S(2)}) copy-start(f32[256]{0:T(256)} %copy-done.86) | copy-start | bytes 3076
  1814.0 181.6 %all-gather.39.cloned.1.call-start = ((), (), s32[]{:S(2)}) async-start(), calls=%async_computation.30 | async-start | bytes 5242880 | tf_op jit(solution)/shard_map/all_gather | solution.py:292
  1895.4 359.9 %reduce-scatter.47.cloned.1.call-start = ((), (), s32[]{:S(2)}) async-start(), calls=%async_computation.39 | async-start | bytes 6488064 | tf_op jit(solution)/shard_map/reduce_scatter | solution.py:337
  1906.1 349.2 %reduce-scatter.45.cloned.1.call-start = ((), (), s32[]{:S(2)}) async-start(), calls=%async_computation.38 | async-start | bytes 6488064 | tf_op jit(solution)/shard_map/reduce_scatter | solution.py:337
  1918.7 340.5 %reduce-scatter.43.cloned.1.call-start = ((), (), s32[]{:S(2)}) async-start(), calls=%async_computation.37 | async-start | bytes 12976128 | tf_op jit(solution)/shard_map/reduce_scatter | solution.py:334
  1953.1 328.6 %reduce-scatter.41.cloned.1.call-start = ((), (), s32[]{:S(2)}) async-start(), calls=%async_computation.36 | async-start | bytes 12976128 | tf_op jit(solution)/shard_map/reduce_scatter | solution.py:334
  1987.7 338.8 %reduce-scatter.39.cloned.1.call-start = ((), (), s32[]{:S(2)}) async-start(), calls=%async_computation.35 | async-start | bytes 2359296 | tf_op jit(solution)/shard_map/reduce_scatter | solution.py:331
  1995.5 375.6 %reduce-scatter.37.cloned.1.call-start = ((), (), s32[]{:S(2)}) async-start(), calls=%async_computation.34 | async-start | bytes 2359296 | tf_op jit(solution)/shard_map/reduce_scatter | solution.py:331
  2001.5 448.7 %reduce-scatter.31.cloned.1.call-start = ((), (), s32[]{:S(2)}) async-start(), calls=%async_computation.31 | async-start | bytes 5242880 | tf_op jit(solution)/shard_map/reduce_scatter | solution.py:315
  2228.3 287.6 %reduce-scatter.35.cloned.1.call-start = ((), (), s32[]{:S(2)}) async-start(), calls=%async_computation.33 | async-start | bytes 7077888 | tf_op jit(solution)/shard_map/reduce_scatter | solution.py:328
  2241.3 340.1 %reduce-scatter.33.cloned.1.call-start = ((), (), s32[]{:S(2)}) async-start(), calls=%async_computation.32 | async-start | bytes 7077888 | tf_op jit(solution)/shard_map/reduce_scatter | solution.py:328
  2254.4 456.5 %all-reduce.3.cloned.1.call-start = ((), (), s32[]{:S(2)}) async-start(), calls=%async_computation.48 | async-start | bytes 229376 | tf_op jit(solution)/shard_map/psum | solution.py:345
  2283.9 166.3 %copy-start.4 = (bf16[256,2048]{1,0:T(8,128)(2,1)S(1)}, bf16[256,2048]{1,0:T(8,128)(2,1)}, u32[]{:S(2)}) copy-start(bf16[256,2048]{1,0:T(8,128)(2,1)} %param.18) | copy-start | bytes 3145732
  2283.9 166.3 %copy-start.64 = (f32[1,1,2048]{2,1,0:T(1,128)S(1)}, f32[1,1,2048]{2,1,0:T(1,128)}, u32[]{:S(2)}) copy-start(f32[1,1,2048]{2,1,0:T(1,128)} %copy-done.63) | copy-start | bytes 24580
  2283.9 166.3 %copy-start.85 = (f32[256]{0:T(256)S(1)}, f32[256]{0:T(256)}, u32[]{:S(2)}) copy-start(f32[256]{0:T(256)} %copy-done.84) | copy-start | bytes 3076
  2283.9 166.3 %copy-start.91 = (f32[256]{0:T(256)S(1)}, f32[256]{0:T(256)}, u32[]{:S(2)}) copy-start(f32[256]{0:T(256)} %copy-done.90) | copy-start | bytes 3076
  2290.9 161.6 %copy-start.75 = (f32[2048]{0:T(1024)S(1)}, f32[2048]{0:T(1024)}, u32[]{:S(2)}) copy-start(f32[2048]{0:T(1024)} %get-tuple-element.313) | copy-start | bytes 24580
  2290.9 161.6 %copy-start.74 = (f32[2048]{0:T(1024)S(1)}, f32[2048]{0:T(1024)}, u32[]{:S(2)}) copy-start(f32[2048]{0:T(1024)} %get-tuple-element.326) | copy-start | bytes 24580
  2290.9 163.0 %copy-start.21 = (f32[256,2048]{1,0:T(8,128)S(1)}, f32[256,2048]{1,0:T(8,128)}, u32[]{:S(2)}) copy-start(f32[256,2048]{1,0:T(8,128)} %get-tuple-element.413) | copy-start | bytes 6291460
  (85 other events, 1325.6 us)
Sparse Core Ops, SparseCore 0:
  16.1 82.8 all-gather.24
  101.5 45.5 all-gather.40
  149.6 28.1 all-gather.42
  214.1 76.3 reduce-scatter.16
  292.9 68.5 all-gather.44
  363.6 80.3 all-gather.26
  446.6 43.2 all-gather.46
  501.0 76.3 reduce-scatter.18
  579.2 47.5 all-gather.48
  628.8 80.3 all-gather.28
  711.1 27.1 all-gather.50
  776.5 75.1 reduce-scatter.20
  853.8 68.5 all-gather.52
  924.5 80.3 all-gather.30
  1006.3 79.2 all-gather.32
  1087.5 43.2 all-gather.54
  1163.9 76.3 reduce-scatter.24
  1242.5 77.2 reduce-scatter.22
  1324.6 81.2 all-gather.34
  1618.4 75.2 reduce-scatter.26
  1699.4 81.2 all-gather.36
  1814.1 75.2 reduce-scatter.28
  1895.5 81.2 all-gather.38
  1980.4 57.5 reduce-scatter.46
  2041.5 59.0 reduce-scatter.44
  2104.3 86.8 reduce-scatter.42
  2194.9 86.7 reduce-scatter.40
  2285.3 41.1 reduce-scatter.38
  2329.9 41.1 reduce-scatter.36
  2373.3 76.8 reduce-scatter.30
  2453.6 62.1 reduce-scatter.34
  2519.6 61.7 reduce-scatter.32
  2587.8 123.0 all-reduce.2
where the time goes:
time: 2740 us; the launch traced here: 2720 us
  waiting for transfers between devices  1740 us (64%)
  matrix products  597 us (22%)
  local copies, waits for them, and re-layouts  255 us (9%)
  other arithmetic  105 us (4%)
    all_gather x4, waiting for transfers between devices, per_device(): lax.all_gather(grad.astype(jnp.bfloat16), 'tensor', axis=0, tiled=True)  225 us
    all_gather x2, waiting for transfers between devices, per_device(): rows_a = lax.all_gather(normed_a, 'tensor', axis=0, tiled=True)  160 us
    reduce_scatter x2, waiting for transfers between devices, per_device(): lax.psum_scatter(back_attn(jnp.int32(0), local_rows * lax.axis_size('tens...  152 us
    reduce_scatter x2, waiting for transfers between devices, per_device(): lax.psum_scatter(project_mlp(jnp.int32(0), local_rows * lax.axis_size('te...  151 us
    reduce_scatter x2, waiting for transfers between devices, per_device(): lax.psum_scatter(project_attn(jnp.int32(0), local_rows * lax.axis_size('t...  143 us
    reduce_scatter x2, waiting for transfers between devices, per_device(): lax.psum_scatter(back_mlp(jnp.int32(0), local_rows * lax.axis_size('tenso...  134 us
    all_gather x2, waiting for transfers between devices, per_device(): rows_b = lax.all_gather(normed_b, 'tensor', axis=0, tiled=True)  134 us
    all_gather x2, waiting for transfers between devices, per_device(): lax.all_gather(w_gate_up[layer_index], 'dp', axis=0, tiled=True)  129 us
  transfers between devices with their start and end apart: 33, of which 27 were waited for; matrix products, arithmetic and copies ran while one was open for 22% of the time, Pallas kernels for 0%

commit v1 on v0

--- a/solution.py
+++ b/solution.py
@@ -196,7 +196,16 @@
         normed_b = (scaled_b * norm_gain[layer_index, 1] + norm_bias[layer_index, 1]).astype(
             jnp.bfloat16
         )
-        rows_b = lax.all_gather(normed_b, "tensor", axis=0, tiled=True)
+        ring = [normed_b]
+        for hop in range(3):
+            ring.append(
+                lax.ppermute(ring[-1], "tensor", [(dev, (dev + 1) % 4) for dev in range(4)])
+            )
+        rows_b = jnp.roll(
+            jnp.concatenate(ring[::-1], axis=0),
+            (lax.axis_index("tensor") + 1) * ring[0].shape[0],
+            axis=0,
+        )
         gate_up = jnp.dot(
             rows_b,
             full_gu.reshape(full_gu.shape[0], 2 * ff_local),

time: 2740 us -> 2590 us (0.945)
  waiting for transfers between devices: 1740 us -> 1550 us
  other arithmetic: 105 us -> 140 us
    all_gather x2 -> x0, waiting for transfers between devices: 134 us -> none  [per_device(): rows_b = lax.all_gather(normed_b, 'tensor', axis=0, tiled=True)]
    ppermute x0 -> x6, waiting for transfers between devices: none -> 99.4 us  [per_device(): lax.ppermute(ring[-1], 'tensor', [(dev, (dev + 1) % 4) for dev in range(4)])]
    all_gather x2, waiting for transfers between devices: 129 us -> 31.5 us  [per_device(): lax.all_gather(w_gate_up[layer_index], 'dp', axis=0, tiled=True)]
    all_gather x4, waiting for transfers between devices: 225 us -> 188 us  [per_device(): lax.all_gather(grad.astype(jnp.bfloat16), 'tensor', axis=0, tiled=True)]
    dynamic_slice x0 -> x2, other arithmetic: none -> 35.6 us  [per_device(): jnp.roll(jnp.concatenate(ring[::-1], axis=0), (lax.axis_index('tensor') +...]
  transfers between devices with their start and end apart: 33 -> 37, of which waited for: 27 -> 28; matrix products, arithmetic and copies ran while one was open for 22% -> 25% of each run, Pallas kernels for 0% -> 0%
where the time goes in v1:
time: 2590 us; the launch traced here: 2570 us
  waiting for transfers between devices  1550 us (60%)
  matrix products  597 us (23%)
  local copies, waits for them, and re-layouts  258 us (10%)
  other arithmetic  140 us (5%)
    all_gather x4, waiting for transfers between devices, per_device(): lax.all_gather(grad.astype(jnp.bfloat16), 'tensor', axis=0, tiled=True)  188 us
    all_gather x2, waiting for transfers between devices, per_device(): rows_a = lax.all_gather(normed_a, 'tensor', axis=0, tiled=True)  161 us
    reduce_scatter x2, waiting for transfers between devices, per_device(): lax.psum_scatter(back_attn(jnp.int32(0), local_rows * lax.axis_size('tens...  153 us
    reduce_scatter x2, waiting for transfers between devices, per_device(): lax.psum_scatter(project_mlp(jnp.int32(0), local_rows * lax.axis_size('te...  151 us
    reduce_scatter x2, waiting for transfers between devices, per_device(): lax.psum_scatter(project_attn(jnp.int32(0), local_rows * lax.axis_size('t...  140 us
    reduce_scatter x2, waiting for transfers between devices, per_device(): lax.psum_scatter(back_mlp(jnp.int32(0), local_rows * lax.axis_size('tenso...  134 us
    psum x1, waiting for transfers between devices, per_device(): lax.psum((jnp.stack(gain_rows), jnp.stack(shift_rows), jnp.stack(qkv_shif...  126 us
    reduce_scatter x2, waiting for transfers between devices, per_device(): lax.psum_scatter(grad_qkv_weight.astype(jnp.bfloat16), 'dp', scatter_dime...  124 us
  transfers between devices with their start and end apart: 37, of which 28 were waited for; matrix products, arithmetic and copies ran while one was open for 25% of the time, Pallas kernels for 0%

profile of v1, /device:TPU:1, one launch (start us, length us, event | category | flops | bytes accessed | tf_op | source)
XLA Modules:
  0.0 2569.5 jit_solution(12648790781538886335)
XLA Ops:
  20.9 78.2 %all-gather.23.cloned.1.call-done = bf16[1024,2048]{1,0:T(8,128)(2,1)} async-done(((bf16[256,2048]{1,0:T(8,128)(2,1)}), bf16[1024,2048]{1,0:T(8,128)(2,1)}) %all-gather.23.cloned.1.call-update) | async-done | bytes 4194320 | tf_op jit(solution)/shard_map/all_gather | solution.py:169
  99.1 48.1 %all-gather.35.cloned.1.call-done = bf16[1,2048,3,512]{1,3,2,0:T(8,128)(2,1)} async-done(((bf16[1,256,3,512]{1,3,2,0:T(8,128)(2,1)}), bf16[1,2048,3,512]{1,3,2,0:T(8,128)(2,1)}) %all-gather.35.cloned.1.call-update) | async-done | bytes 6291472 | tf_op jit(solution)/shard_map/all_gather | solution.py:159
  171.8 31.3 %while.54 = (s32[]{:T(128)}, bf16[2,512,8,64]{1,3,2,0:T(8,128)(2,1)}, f32[2,8,512,1]{2,1,3,0:T(8,128)S(1)}, s32[2]{0:T(128)S(1)}, s32[1024]{0:T(1024)S(1)}, /*in...) while((s32[]{:T(128)}, ...), condition=%wide.region_5.6_spmd, body=%wide.region_2.5_spmd.sunk | while | flops 1125643264 | bytes 64628996 | solution.py:94
  221.8 68.5 %reduce-scatter.17.cloned.1.call-done = bf16[256,2048]{1,0:T(8,128)(2,1)} async-done(((bf16[1024,2048]{1,0:T(8,128)(2,1)}), bf16[256,2048]{1,0:T(8,128)(2,1)}) %reduce-scatter.17.cloned.1.call-update) | async-done | bytes 1048592 | tf_op jit(solution)/shard_map/reduce_scatter | solution.py:188
  295.7 24.7 collective-permute-done
  321.3 25.1 collective-permute-done.1
  390.4 17.6 fusion.96
  428.6 74.2 %reduce-scatter.19.cloned.1.call-done = bf16[256,2048]{1,0:T(8,128)(2,1)} async-done(((bf16[1024,2048]{1,0:T(8,128)(2,1)}), bf16[256,2048]{1,0:T(8,128)(2,1)}) %reduce-scatter.19.cloned.1.call-update) | async-done | bytes 1048592 | tf_op jit(solution)/shard_map/reduce_scatter | solution.py:219
  508.6 43.6 %all-gather.43.cloned.1.call-done = bf16[1,2048,3,512]{1,3,2,0:T(8,128)(2,1)} async-done(((bf16[1,256,3,512]{1,3,2,0:T(8,128)(2,1)}), bf16[1,2048,3,512]{1,3,2,0:T(8,128)(2,1)}) %all-gather.43.cloned.1.call-update) | async-done | bytes 6291472 | tf_op jit(solution)/shard_map/all_gather | solution.py:159
  552.3 82.5 %all-gather.25.cloned.1.call-done = bf16[1024,2048]{1,0:T(8,128)(2,1)} async-done(((bf16[256,2048]{1,0:T(8,128)(2,1)}), bf16[1024,2048]{1,0:T(8,128)(2,1)}) %all-gather.25.cloned.1.call-update) | async-done | bytes 4194320 | tf_op jit(solution)/shard_map/all_gather | solution.py:169
  660.4 33.8 %while.55 = (s32[]{:T(128)}, bf16[2,512,8,64]{1,3,2,0:T(8,128)(2,1)S(1)}, f32[2,8,512,1]{2,1,3,0:T(8,128)S(1)}, s32[2]{0:T(128)S(1)}, s32[1024]{0:T(1024)S(1)}, ...) while((s32[]{:T(128)}, ...), condition=%wide.region_15.17_spmd, body=%wide.region_12.16_spmd.sunk | while | flops 1125643264 | bytes 56240328 | solution.py:94
  706.0 71.3 %reduce-scatter.21.cloned.1.call-done = bf16[256,2048]{1,0:T(8,128)(2,1)} async-done(((bf16[1024,2048]{1,0:T(8,128)(2,1)}), bf16[256,2048]{1,0:T(8,128)(2,1)}) %reduce-scatter.21.cloned.1.call-update) | async-done | bytes 1048592 | tf_op jit(solution)/shard_map/reduce_scatter | solution.py:188
  781.9 24.7 collective-permute-done.3
  806.5 24.9 collective-permute-done.4
  831.5 16.4 all-gather.47.cloned.1.call-done
  863.3 22.1 fusion.122
  887.4 17.5 fusion.94
  904.9 25.0 all-gather.27.cloned.1.call-done
  929.9 45.2 %all-gather.49.cloned.1.call-done = bf16[1,1408,2048]{2,1,0:T(8,128)(2,1)} async-done(((bf16[1,1408,256]{2,1,0:T(8,128)(2,1)}), bf16[1,1408,2048]{2,1,0:T(8,128)(2,1)}) %all-gather.49.cloned.1.call-update) | async-done | bytes 5767184 | tf_op jit(solution)/shard_map/all_gather | solution.py:162
  1026.1 58.7 %reduce-scatter.25.cloned.1.call-done = bf16[256,2048]{1,0:T(8,128)(2,1)} async-done(((bf16[1024,2048]{1,0:T(8,128)(2,1)}), bf16[256,2048]{1,0:T(8,128)(2,1)}) %reduce-scatter.25.cloned.1.call-update) | async-done | bytes 1048592 | tf_op jit(solution)/shard_map/reduce_scatter | solution.py:291
  1087.6 76.7 %reduce-scatter.23.cloned.1.call-done = bf16[256,2048]{1,0:T(8,128)(2,1)} async-done(((bf16[1024,2048]{1,0:T(8,128)(2,1)}), bf16[256,2048]{1,0:T(8,128)(2,1)}) %reduce-scatter.23.cloned.1.call-update) | async-done | bytes 1048592 | tf_op jit(solution)/shard_map/reduce_scatter | solution.py:219
  1169.1 81.3 %all-gather.29.cloned.1.call-done = bf16[1024,2048]{1,0:T(8,128)(2,1)} async-done(((bf16[256,2048]{1,0:T(8,128)(2,1)}), bf16[1024,2048]{1,0:T(8,128)(2,1)}) %all-gather.29.cloned.1.call-update) | async-done | bytes 4194320 | tf_op jit(solution)/shard_map/all_gather | solution.py:301
  1258.6 183.8 %while.56 = (s32[]{:T(128)}, f32[1024,8,64]{0,2,1:T(8,128)}, f32[1024,8,64]{0,2,1:T(8,128)S(1)}, f32[2,512,8,64]{1,0,3,2:T(2,128)}, s32[2]{0:T(128)S(1)}, /*inde...) while((s32[]{:T(128)}, f32[1024,8,64]{0,2,1:T(8,128)}, ...), condition=%wide.region_25.27_spmd.clone, body=%wide.region_23.26_spmd.clone.sunk | while | flops 2747542528 | bytes 239134992 | solution.py:138
  1282.0 22.9 fusion.318
  1305.0 23.3 bitcast_add_fusion.8
  1330.6 19.6 dynamic_update_slice.48
  1373.4 22.9 fusion.318
  1396.4 23.9 bitcast_add_fusion.8
  1422.6 19.6 dynamic_update_slice.48
  1462.9 75.4 %reduce-scatter.27.cloned.1.call-done = bf16[256,2048]{1,0:T(8,128)(2,1)} async-done(((bf16[1024,2048]{1,0:T(8,128)(2,1)}), bf16[256,2048]{1,0:T(8,128)(2,1)}) %reduce-scatter.27.cloned.1.call-update) | async-done | bytes 1048592 | tf_op jit(solution)/shard_map/reduce_scatter | solution.py:324
  1545.2 81.3 %all-gather.31.cloned.1.call-done = bf16[1024,2048]{1,0:T(8,128)(2,1)} async-done(((bf16[256,2048]{1,0:T(8,128)(2,1)}), bf16[1024,2048]{1,0:T(8,128)(2,1)}) %all-gather.31.cloned.1.call-update) | async-done | bytes 4194320 | tf_op jit(solution)/shard_map/all_gather | solution.py:272
  1659.8 75.4 %reduce-scatter.29.cloned.1.call-done = bf16[256,2048]{1,0:T(8,128)(2,1)} async-done(((bf16[1024,2048]{1,0:T(8,128)(2,1)}), bf16[256,2048]{1,0:T(8,128)(2,1)}) %reduce-scatter.29.cloned.1.call-update) | async-done | bytes 1048592 | tf_op jit(solution)/shard_map/reduce_scatter | solution.py:291
  1780.9 19.1 convolution_convert_fusion
  1815.4 19.2 convolution_convert_fusion.1
  1857.9 199.0 %while.57 = (s32[]{:T(128)}, f32[1024,8,64]{0,2,1:T(8,128)}, f32[1024,8,64]{0,2,1:T(8,128)}, f32[2,512,8,64]{1,0,3,2:T(2,128)}, s32[2]{0:T(128)S(1)}, /*index=5*...) while((s32[]{:T(128)}, f32[1024,8,64]{0,2,1:T(8,128)}, ...), condition=%wide.region_34.36_spmd.clone, body=%wide.region_32.35_spmd.clone.sunk | while | flops 2747542528 | bytes 239134992 | solution.py:138
  1881.5 27.7 %fusion.331 = f32[1,512,8,64]{1,3,2,0:T(8,128)} fusion(bf16[1024,8,64]{0,2,1:T(8,128)(2,1)S(1)} %get-tuple-element.901, f32[8,512,1024]{2,1,0:T(8,128)} %copy-done.1, f32[8,512,1024]{2,1,0:T(8,128)} %fusion.330, pred[512,1024]{1,0:T(8,128)(4,1)S(1)} %fusion.329), kind=kOutput, calls=%fused_computation.87.clone.1 | convolution fusion | flops 558109696 | bytes 36175872 | tf_op jit(solution)/shard_map/while/body/eval_jaxpr/hqk,khd->qhd/dot_general | solution.py:124
  1909.3 24.7 bitcast_add_fusion.10
  1936.3 19.5 dynamic_update_slice.49
  1982.3 27.3 %fusion.331 = f32[1,512,8,64]{1,3,2,0:T(8,128)} fusion(bf16[1024,8,64]{0,2,1:T(8,128)(2,1)S(1)} %get-tuple-element.901, f32[8,512,1024]{2,1,0:T(8,128)} %copy-done.1, f32[8,512,1024]{2,1,0:T(8,128)} %fusion.330, pred[512,1024]{1,0:T(8,128)(4,1)S(1)} %fusion.329), kind=kOutput, calls=%fused_computation.87.clone.1 | convolution fusion | flops 558109696 | bytes 36175872 | tf_op jit(solution)/shard_map/while/body/eval_jaxpr/hqk,khd->qhd/dot_general | solution.py:124
  2009.6 25.3 bitcast_add_fusion.10
  2037.2 19.7 dynamic_update_slice.49
  2107.3 21.7 reduce-scatter.41.cloned.1.call-done
  2138.2 35.5 %reduce-scatter.39.cloned.1.call-done = bf16[512,256]{1,0:T(8,128)(2,1)} async-done(((bf16[512,2048]{1,0:T(8,128)(2,1)}), bf16[512,256]{1,0:T(8,128)(2,1)}) %reduce-scatter.39.cloned.1.call-update) | async-done | bytes 262160 | tf_op jit(solution)/shard_map/reduce_scatter | solution.py:340
  2173.7 44.4 %reduce-scatter.37.cloned.1.call-done = bf16[512,256]{1,0:T(8,128)(2,1)} async-done(((bf16[512,2048]{1,0:T(8,128)(2,1)}), bf16[512,256]{1,0:T(8,128)(2,1)}) %reduce-scatter.37.cloned.1.call-update) | async-done | bytes 262160 | tf_op jit(solution)/shard_map/reduce_scatter | solution.py:340
  2220.2 77.1 %reduce-scatter.31.cloned.1.call-done = bf16[256,2048]{1,0:T(8,128)(2,1)} async-done(((bf16[1024,2048]{1,0:T(8,128)(2,1)}), bf16[256,2048]{1,0:T(8,128)(2,1)}) %reduce-scatter.31.cloned.1.call-update) | async-done | bytes 1048592 | tf_op jit(solution)/shard_map/reduce_scatter | solution.py:324
  2304.4 58.6 %reduce-scatter.35.cloned.1.call-done = bf16[256,3,512]{2,0,1:T(8,128)(2,1)} async-done(((bf16[2048,3,512]{2,0,1:T(8,128)(2,1)}), bf16[256,3,512]{2,0,1:T(8,128)(2,1)}) %reduce-scatter.35.cloned.1.call-update) | async-done | bytes 786448 | tf_op jit(solution)/shard_map/reduce_scatter | solution.py:337
  2363.0 65.4 %reduce-scatter.33.cloned.1.call-done = bf16[256,3,512]{2,0,1:T(8,128)(2,1)} async-done(((bf16[2048,3,512]{2,0,1:T(8,128)(2,1)}), bf16[256,3,512]{2,0,1:T(8,128)(2,1)}) %reduce-scatter.33.cloned.1.call-update) | async-done | bytes 786448 | tf_op jit(solution)/shard_map/reduce_scatter | solution.py:337
  2431.6 126.4 %all-reduce.3.cloned.1.call-done = (f32[2,2,2048]{2,1,0:T(2,128)}, f32[2,2,2048]{2,1,0:T(2,128)}, f32[2,3,2048]{2,0,1:T(2,128)}) async-done(((f32[2,2,2048]{2,1,0:T(2,128)}, f32[2,2,2048]{2,1,0:T(2,128)}, f32[2,3,2048]{2,0,1:T(2,128)}), (f32[2,2,2048]{2,1,0:T(2,128)}, f32[2,2,2048]{2,1,0:T(2,128)}, f32[2,3,2048]{2,0,1:T(2,128)})) %all-reduce.3.cloned.1.call-update) | async-done | bytes 114704 | tf_op jit(solution)/shard_map/psum | solution.py:354
  (495 shorter events, 644.3 us)
Async XLA Ops:
  7.2 91.9 %all-gather.23.cloned.1.call-start = ((), (), s32[]{:S(2)}) async-start(), calls=%async_computation.16 | async-start | bytes 5242880 | tf_op jit(solution)/shard_map/all_gather | solution.py:169
  16.1 131.1 %all-gather.35.cloned.1.call-start = ((), (), s32[]{:S(2)}) async-start(), calls=%async_computation.38 | async-start | bytes 7077888 | tf_op jit(solution)/shard_map/all_gather | solution.py:159
  18.4 189.1 %all-gather.37.cloned.1.call-start = ((), (), s32[]{:S(2)}) async-start(), calls=%async_computation.39 | async-start | bytes 2359296 | tf_op jit(solution)/shard_map/all_gather | solution.py:160
  19.3 271.1 %reduce-scatter.17.cloned.1.call-start = ((), (), s32[]{:S(2)}) async-start(), calls=%async_computation.17 | async-start | bytes 5242880 | tf_op jit(solution)/shard_map/reduce_scatter | solution.py:188
  20.9 149.5 %copy-start.48 = (f32[1024,8]{0,1:T(8,128)}, f32[1024,8]{0,1:T(8,128)S(1)}, u32[]{:S(2)}) copy-start(f32[1024,8]{0,1:T(8,128)S(1)} %get-tuple-element.488) | copy-start | bytes 98308
  20.9 149.5 %copy-start.62 = (f32[1024,8]{0,1:T(8,128)}, f32[1024,8]{0,1:T(8,128)S(1)}, u32[]{:S(2)}) copy-start(f32[1024,8]{0,1:T(8,128)S(1)} %get-tuple-element.487) | copy-start | bytes 98308
  213.9 147.6 %all-gather.39.cloned.1.call-start = ((), (), s32[]{:S(2)}) async-start(), calls=%async_computation.40 | async-start | bytes 12976128 | tf_op jit(solution)/shard_map/all_gather | solution.py:161
  219.8 195.5 %all-gather.41.cloned.1.call-start = ((), (), s32[]{:S(2)}) async-start(), calls=%async_computation.41 | async-start | bytes 6488064 | tf_op jit(solution)/shard_map/all_gather | solution.py:162
  221.8 281.0 %reduce-scatter.19.cloned.1.call-start = ((), (), s32[]{:S(2)}) async-start(), calls=%async_computation.18 | async-start | bytes 5242880 | tf_op jit(solution)/shard_map/reduce_scatter | solution.py:219
  294.4 25.9 %collective-permute-start = (bf16[256,2048]{1,0:T(8,128)(2,1)S(1)}, bf16[256,2048]{1,0:T(8,128)(2,1)S(1)}, u32[]{:S(2)}, u32[]{:S(2)}) collective-permute-start(bf16[256,2048]{1,0:T(8,128)(2,1)S(1)} %add_convert_fusion.3), channel_id=1, source_target_pairs={{0,1},{1,2},{2,3},{3,0},{4,5},{5,6},{6,7},{7,4},{8,9},{9,10},{10,1... | collective-permute-start | bytes 3145736 | tf_op jit(solution)/shard_map/ppermute | solution.py:202
  321.3 25.1 collective-permute-start.1
  346.4 30.5 %collective-permute-start.2 = (bf16[256,2048]{1,0:T(8,128)(2,1)}, bf16[256,2048]{1,0:T(8,128)(2,1)}, u32[]{:S(2)}, u32[]{:S(2)}) collective-permute-start(bf16[256,2048]{1,0:T(8,128)(2,1)} %collective-permute-done.1), channel_id=1, source_target_pairs={{0,1},{1,2},{2,3},{3,0},{4,5},{5,6},{6,7},{7,4},{8,9},{9,10},{10,1... | collective-permute-start | bytes 3145736 | tf_op jit(solution)/shard_map/ppermute | solution.py:202
  426.2 126.0 %all-gather.43.cloned.1.call-start = ((), (), s32[]{:S(2)}) async-start(), calls=%async_computation.42 | async-start | bytes 7077888 | tf_op jit(solution)/shard_map/all_gather | solution.py:159
  428.6 206.2 %all-gather.25.cloned.1.call-start = ((), (), s32[]{:S(2)}) async-start(), calls=%async_computation.19 | async-start | bytes 5242880 | tf_op jit(solution)/shard_map/all_gather | solution.py:169
  504.5 142.1 %copy-start.84 = (f32[256]{0:T(256)}, f32[256]{0:T(256)S(1)}, u32[]{:S(2)}) copy-start(f32[256]{0:T(256)S(1)} %broadcast_multiply_fusion.9) | copy-start | bytes 3076
  504.9 141.7 %copy-start.90 = (f32[256]{0:T(256)}, f32[256]{0:T(256)S(1)}, u32[]{:S(2)}) copy-start(f32[256]{0:T(256)S(1)} %add_rsqrt_fusion.1) | copy-start | bytes 3076
  507.3 188.3 %all-gather.45.cloned.1.call-start = ((), (), s32[]{:S(2)}) async-start(), calls=%async_computation.43 | async-start | bytes 2359296 | tf_op jit(solution)/shard_map/all_gather | solution.py:160
  507.9 269.4 %reduce-scatter.21.cloned.1.call-start = ((), (), s32[]{:S(2)}) async-start(), calls=%async_computation.20 | async-start | bytes 5242880 | tf_op jit(solution)/shard_map/reduce_scatter | solution.py:188
  702.0 145.9 %all-gather.47.cloned.1.call-start = ((), (), s32[]{:S(2)}) async-start(), calls=%async_computation.44 | async-start | bytes 12976128 | tf_op jit(solution)/shard_map/all_gather | solution.py:161
  704.6 225.3 %all-gather.27.cloned.1.call-start = ((), (), s32[]{:S(2)}) async-start(), calls=%async_computation.22 | async-start | bytes 5242880 | tf_op jit(solution)/shard_map/all_gather | solution.py:272
  705.4 269.7 %all-gather.49.cloned.1.call-start = ((), (), s32[]{:S(2)}) async-start(), calls=%async_computation.45 | async-start | bytes 6488064 | tf_op jit(solution)/shard_map/all_gather | solution.py:162
  706.0 378.9 %reduce-scatter.25.cloned.1.call-start = ((), (), s32[]{:S(2)}) async-start(), calls=%async_computation.23 | async-start | bytes 5242880 | tf_op jit(solution)/shard_map/reduce_scatter | solution.py:291
  780.6 25.9 %collective-permute-start.3 = (bf16[256,2048]{1,0:T(8,128)(2,1)S(1)}, bf16[256,2048]{1,0:T(8,128)(2,1)S(1)}, u32[]{:S(2)}, u32[]{:S(2)}) collective-permute-start(bf16[256,2048]{1,0:T(8,128)(2,1)S(1)} %add_convert_fusion.1), channel_id=1, source_target_pairs={{0,1},{1,2},{2,3},{3,0},{4,5},{5,6},{6,7},{7,4},{8,9},{9,10},{10,1... | collective-permute-start | bytes 3145736 | tf_op jit(solution)/shard_map/ppermute | solution.py:202
  806.5 25.0 collective-permute-start.4
  831.5 31.8 %collective-permute-start.5 = (bf16[256,2048]{1,0:T(8,128)(2,1)S(1)}, bf16[256,2048]{1,0:T(8,128)(2,1)}, u32[]{:S(2)}, u32[]{:S(2)}) collective-permute-start(bf16[256,2048]{1,0:T(8,128)(2,1)S(1)} %collective-permute-done.4), channel_id=1, source_target_pairs={{0,1},{1,2},{2,3},{3,0},{4,5},{5,6},{6,7},{7,4},{8,9},{9,10},{10,1... | collective-permute-start | bytes 3145736 | tf_op jit(solution)/shard_map/ppermute | solution.py:202
  1008.3 156.0 %reduce-scatter.23.cloned.1.call-start = ((), (), s32[]{:S(2)}) async-start(), calls=%async_computation.21 | async-start | bytes 5242880 | tf_op jit(solution)/shard_map/reduce_scatter | solution.py:219
  1026.1 224.3 %all-gather.29.cloned.1.call-start = ((), (), s32[]{:S(2)}) async-start(), calls=%async_computation.24 | async-start | bytes 5242880 | tf_op jit(solution)/shard_map/all_gather | solution.py:301
  1169.0 369.4 %reduce-scatter.27.cloned.1.call-start = ((), (), s32[]{:S(2)}) async-start(), calls=%async_computation.25 | async-start | bytes 5242880 | tf_op jit(solution)/shard_map/reduce_scatter | solution.py:324
  1462.9 163.6 %all-gather.31.cloned.1.call-start = ((), (), s32[]{:S(2)}) async-start(), calls=%async_computation.26 | async-start | bytes 5242880 | tf_op jit(solution)/shard_map/all_gather | solution.py:272
  1545.1 190.1 %reduce-scatter.29.cloned.1.call-start = ((), (), s32[]{:S(2)}) async-start(), calls=%async_computation.27 | async-start | bytes 5242880 | tf_op jit(solution)/shard_map/reduce_scatter | solution.py:291
  1659.8 182.8 %all-gather.33.cloned.1.call-start = ((), (), s32[]{:S(2)}) async-start(), calls=%async_computation.28 | async-start | bytes 5242880 | tf_op jit(solution)/shard_map/all_gather | solution.py:301
  1742.4 360.9 %reduce-scatter.47.cloned.1.call-start = ((), (), s32[]{:S(2)}) async-start(), calls=%async_computation.37 | async-start | bytes 6488064 | tf_op jit(solution)/shard_map/reduce_scatter | solution.py:346
  1753.1 350.2 %reduce-scatter.45.cloned.1.call-start = ((), (), s32[]{:S(2)}) async-start(), calls=%async_computation.36 | async-start | bytes 6488064 | tf_op jit(solution)/shard_map/reduce_scatter | solution.py:346
  1765.7 341.6 %reduce-scatter.43.cloned.1.call-start = ((), (), s32[]{:S(2)}) async-start(), calls=%async_computation.35 | async-start | bytes 12976128 | tf_op jit(solution)/shard_map/reduce_scatter | solution.py:343
  1800.1 329.0 %reduce-scatter.41.cloned.1.call-start = ((), (), s32[]{:S(2)}) async-start(), calls=%async_computation.34 | async-start | bytes 12976128 | tf_op jit(solution)/shard_map/reduce_scatter | solution.py:343
  1834.7 339.1 %reduce-scatter.39.cloned.1.call-start = ((), (), s32[]{:S(2)}) async-start(), calls=%async_computation.33 | async-start | bytes 2359296 | tf_op jit(solution)/shard_map/reduce_scatter | solution.py:340
  1842.4 375.7 %reduce-scatter.37.cloned.1.call-start = ((), (), s32[]{:S(2)}) async-start(), calls=%async_computation.32 | async-start | bytes 2359296 | tf_op jit(solution)/shard_map/reduce_scatter | solution.py:340
  1848.5 448.8 %reduce-scatter.31.cloned.1.call-start = ((), (), s32[]{:S(2)}) async-start(), calls=%async_computation.29 | async-start | bytes 5242880 | tf_op jit(solution)/shard_map/reduce_scatter | solution.py:324
  2076.1 286.9 %reduce-scatter.35.cloned.1.call-start = ((), (), s32[]{:S(2)}) async-start(), calls=%async_computation.31 | async-start | bytes 7077888 | tf_op jit(solution)/shard_map/reduce_scatter | solution.py:337
  2089.4 339.0 %reduce-scatter.33.cloned.1.call-start = ((), (), s32[]{:S(2)}) async-start(), calls=%async_computation.30 | async-start | bytes 7077888 | tf_op jit(solution)/shard_map/reduce_scatter | solution.py:337
  2102.4 455.6 %all-reduce.3.cloned.1.call-start = ((), (), s32[]{:S(2)}) async-start(), calls=%async_computation.46 | async-start | bytes 229376 | tf_op jit(solution)/shard_map/psum | solution.py:354
  2131.2 166.2 %copy-start.4 = (bf16[256,2048]{1,0:T(8,128)(2,1)S(1)}, bf16[256,2048]{1,0:T(8,128)(2,1)}, u32[]{:S(2)}) copy-start(bf16[256,2048]{1,0:T(8,128)(2,1)} %param.20) | copy-start | bytes 3145732
  2131.2 166.2 %copy-start.65 = (f32[1,1,2048]{2,1,0:T(1,128)S(1)}, f32[1,1,2048]{2,1,0:T(1,128)}, u32[]{:S(2)}) copy-start(f32[1,1,2048]{2,1,0:T(1,128)} %copy-done.64) | copy-start | bytes 24580
  2131.2 166.2 %copy-start.87 = (f32[256]{0:T(256)S(1)}, f32[256]{0:T(256)}, u32[]{:S(2)}) copy-start(f32[256]{0:T(256)} %copy-done.86) | copy-start | bytes 3076
  2131.2 166.1 %copy-start.93 = (f32[256]{0:T(256)S(1)}, f32[256]{0:T(256)}, u32[]{:S(2)}) copy-start(f32[256]{0:T(256)} %copy-done.92) | copy-start | bytes 3076
  2131.2 168.4 %copy-start.76 = (f32[2048]{0:T(1024)S(1)}, f32[2048]{0:T(1024)}, u32[]{:S(2)}) copy-start(f32[2048]{0:T(1024)} %get-tuple-element.314) | copy-start | bytes 24580
  2131.2 168.5 %copy-start.75 = (f32[2048]{0:T(1024)S(1)}, f32[2048]{0:T(1024)}, u32[]{:S(2)}) copy-start(f32[2048]{0:T(1024)} %get-tuple-element.327) | copy-start | bytes 24580
  2138.2 162.8 %copy-start.21 = (f32[256,2048]{1,0:T(8,128)S(1)}, f32[256,2048]{1,0:T(8,128)}, u32[]{:S(2)}) copy-start(f32[256,2048]{1,0:T(8,128)} %get-tuple-element.414) | copy-start | bytes 6291460
  (91 other events, 2033.5 us)
Sparse Core Ops, SparseCore 0:
  16.2 82.8 all-gather.22
  101.5 45.5 all-gather.34
  149.6 28.1 all-gather.36
  214.0 76.3 reduce-scatter.16
  292.9 68.5 all-gather.38
  363.4 44.3 all-gather.40
  426.4 76.3 reduce-scatter.18
  504.7 47.5 all-gather.42
  554.4 80.3 all-gather.24
  636.5 27.1 all-gather.44
  702.1 75.1 reduce-scatter.20
  779.2 68.5 all-gather.46
  849.5 80.3 all-gather.26
  931.8 43.2 all-gather.48
  1008.4 76.3 reduce-scatter.24
  1087.0 77.2 reduce-scatter.22
  1169.1 81.2 all-gather.28
  1463.0 75.3 reduce-scatter.26
  1545.2 81.2 all-gather.30
  1659.9 75.3 reduce-scatter.28
  1742.5 81.2 all-gather.32
  1827.6 57.5 reduce-scatter.46
  1888.6 59.0 reduce-scatter.44
  1951.5 86.7 reduce-scatter.42
  2042.2 86.7 reduce-scatter.40
  2132.5 41.1 reduce-scatter.38
  2176.9 41.2 reduce-scatter.36
  2220.5 76.7 reduce-scatter.30
  2300.7 62.2 reduce-scatter.34
  2366.6 61.7 reduce-scatter.32
  2434.9 123.0 all-reduce.2
